TPU v7x, 32 devices: a whole 2x2x4 slice. The times are simulated.
32 devices in a mesh: dp: 8 (over z, y), sp: 4 (over x, core).
Axes of the slice: x: 2, y: 2, z: 4, core: 2. Of those that a mesh axis runs over, the one named last changes fastest.
Arguments:
- tokens: bfloat16 [16, 1024, 512], P('dp', 'sp'), may hold values from -6 to 6
- lengths: int32 [16], P('dp'), may hold values from 64 to 1024, as said below
- post_query: bfloat16 [512, 512], replicated, may hold values from -0.25 to 0.25
- post_key: bfloat16 [512, 512], replicated, may hold values from -0.25 to 0.25
- post_value: bfloat16 [512, 512], replicated, may hold values from -0.25 to 0.25
- post_out: bfloat16 [512, 512], replicated, may hold values from -1 to 1
- post_gate: bfloat16 [512, 1376], replicated, may hold values from -0.25 to 0.25
- post_up: bfloat16 [512, 1376], replicated, may hold values from -0.25 to 0.25
- post_down: bfloat16 [1376, 512], replicated, may hold values from -0.15625 to 0.15625
- post_attn_gain: float32 [512], replicated, may hold values from 0.5 to 1.5
- post_ffn_gain: float32 [512], replicated, may hold values from 0.5 to 1.5
- pre_query: bfloat16 [512, 512], replicated, may hold values from -0.25 to 0.25
- pre_key: bfloat16 [512, 512], replicated, may hold values from -0.25 to 0.25
- pre_value: bfloat16 [512, 512], replicated, may hold values from -0.25 to 0.25
- pre_out: bfloat16 [512, 512], replicated, may hold values from -1 to 1
- pre_gate: bfloat16 [512, 1376], replicated, may hold values from -0.25 to 0.25
- pre_up: bfloat16 [512, 1376], replicated, may hold values from -0.25 to 0.25
- pre_down: bfloat16 [1376, 512], replicated, may hold values from -0.15625 to 0.15625
- pre_attn_gain: float32 [512], replicated, may hold values from 0.5 to 1.5
- pre_ffn_gain: float32 [512], replicated, may hold values from 0.5 to 1.5
- out_grad: bfloat16 [16, 1024, 512], P('dp', 'sp'), may hold values from -6 to 6
Outputs:
- output: bfloat16 [16, 1024, 512], P('dp', 'sp')
- tokens_grad: bfloat16 [16, 1024, 512], P('dp', 'sp')
- grad_post_query: float32 [512, 512], replicated
- grad_post_key: float32 [512, 512], replicated
- grad_post_value: float32 [512, 512], replicated
- grad_post_out: float32 [512, 512], replicated
- grad_post_gate: float32 [512, 1376], replicated
- grad_post_up: float32 [512, 1376], replicated
- grad_post_down: float32 [1376, 512], replicated
- grad_post_attn_gain: float32 [512], replicated
- grad_post_ffn_gain: float32 [512], replicated
- grad_pre_query: float32 [512, 512], replicated
- grad_pre_key: float32 [512, 512], replicated
- grad_pre_value: float32 [512, 512], replicated
- grad_pre_out: float32 [512, 512], replicated
- grad_pre_gate: float32 [512, 1376], replicated
- grad_pre_up: float32 [512, 1376], replicated
- grad_pre_down: float32 [1376, 512], replicated
- grad_pre_attn_gain: float32 [512], replicated
- grad_pre_ffn_gain: float32 [512], replicated
Inputs may be any that keep to these rules, and one draw needn't show every extreme that they name: `lengths`: some slot has length exactly 1024 and some exactly 64.
All inputs are finite; a program needn't handle non-finite values.
Results may differ from a plain program's by a relative error of at most 0.024.
Values may be sent and summed in bfloat16 or wider, within the bound.
No kernel may reach another device: no remote copies, remote signals or barrier semaphores. Data moves between devices by JAX's collectives and lax.ppermute only.
A program may use at most 192 MiB of HBM per device.

v0:
```python
import jax
import jax.numpy as jnp
from jax import lax
from jax.sharding import PartitionSpec as P

HEADS = 8
HD = 64
SEQ = 1024
eps = 1e-06


def norm_rows(values, gain_vec):
    return values * lax.rsqrt(jnp.mean(values * values, axis=-1, keepdims=True) + eps) * gain_vec


def rotary_tables(start, row_count):
    half_dim = HD // 2
    inverse = 10000.0 ** (-jnp.arange(half_dim, dtype=jnp.float32) * 2.0 / HD)
    positions = (start + jnp.arange(row_count, dtype=jnp.int32)).astype(jnp.float32)
    angles = positions[:, None] * inverse[None, :]
    cosine = jnp.concatenate([jnp.cos(angles), jnp.cos(angles)], axis=-1)
    sine_table = jnp.concatenate([jnp.sin(angles), jnp.sin(angles)], axis=-1)
    return (cosine, sine_table)


def rotate(values, cosine, sine_table):
    half_dim = values.shape[-1] // 2
    turned = jnp.concatenate([-values[..., half_dim:], values[..., :half_dim]], axis=-1)
    return values * cosine[:, None, :] + turned * sine_table[:, None, :]


def rotate_back(grads, cosine, sine_table):
    half_dim = grads.shape[-1] // 2
    turned = grads * sine_table[:, None, :]
    backward = jnp.concatenate([turned[..., half_dim:], -turned[..., :half_dim]], axis=-1)
    return grads * cosine[:, None, :] + backward


def gated(gate_act, up_act):
    return jax.nn.silu(gate_act) * up_act


def slot_scores(queries, key_heads, length):
    scores = jnp.einsum(
        "qhd,khd->hqk", queries, key_heads, preferred_element_type=jnp.float32
    ) * HD ** (-0.5)
    row_index = jnp.arange(SEQ, dtype=jnp.int32)[:, None]
    col_index = jnp.arange(SEQ, dtype=jnp.int32)[None, :]
    allowed = (col_index <= row_index) & (col_index < length)
    return jnp.where(allowed[None], scores, -1000000000.0)


def attend_slot(pieces):
    queries, key_heads, value_heads, length = pieces
    scores = slot_scores(queries, key_heads, length)
    maxima = jnp.max(scores, axis=-1, keepdims=True)
    log_total = maxima + jnp.log(jnp.sum(jnp.exp(scores - maxima), axis=-1, keepdims=True))
    softmax_p = jnp.exp(scores - log_total)
    mixed_heads = jnp.einsum(
        "hqk,khd->qhd",
        softmax_p.astype(jnp.bfloat16),
        value_heads,
        preferred_element_type=jnp.float32,
    )
    return (mixed_heads.astype(jnp.bfloat16), log_total)


def attend_back(pieces):
    queries, key_heads, value_heads, log_total, grad_mixed, length = pieces
    softmax_p = jnp.exp(slot_scores(queries, key_heads, length) - log_total)
    grad_values = jnp.einsum(
        "hqk,qhd->khd",
        softmax_p.astype(jnp.bfloat16),
        grad_mixed,
        preferred_element_type=jnp.float32,
    )
    grad_probs = jnp.einsum(
        "qhd,khd->hqk", grad_mixed, value_heads, preferred_element_type=jnp.float32
    )
    row_delta = jnp.sum(softmax_p * grad_probs, axis=-1, keepdims=True)
    grad_scores = (softmax_p * (grad_probs - row_delta)).astype(jnp.bfloat16)
    grad_queries = jnp.einsum(
        "hqk,khd->qhd", grad_scores, key_heads, preferred_element_type=jnp.float32
    ) * HD ** (-0.5)
    grad_keys = jnp.einsum(
        "hqk,qhd->khd", grad_scores, queries, preferred_element_type=jnp.float32
    ) * HD ** (-0.5)
    return (
        grad_queries.astype(jnp.bfloat16),
        grad_keys.astype(jnp.bfloat16),
        grad_values.astype(jnp.bfloat16),
    )


def layer_forward(inputs, weights, lengths, post_norm, cosine, sine_table):
    w_query, w_key, w_value, w_out, w_gate, w_up, w_down, gain_att, gain_ffn = weights
    group = lax.axis_size("sp")
    slot_count, row_count, width = inputs.shape
    local_heads = HEADS // group
    full_rows = row_count * group
    if post_norm:
        entry_rows = inputs.astype(jnp.bfloat16)
    else:
        entry_rows = norm_rows(inputs, gain_att).astype(jnp.bfloat16)

    def rotated(weight):
        product = jnp.einsum("nsd,de->nse", entry_rows, weight, preferred_element_type=jnp.float32)
        turned = rotate(product.reshape(slot_count, row_count, HEADS, HD), cosine, sine_table)
        return turned.astype(jnp.bfloat16).reshape(slot_count, row_count, group, local_heads * HD)

    query_rows = rotated(w_query)
    key_rows = rotated(w_key)
    value_rows = jnp.einsum("nsd,de->nse", entry_rows, w_value, preferred_element_type=jnp.float32)
    value_rows = value_rows.astype(jnp.bfloat16).reshape(
        slot_count, row_count, group, local_heads * HD
    )
    query_heads, key_heads, value_heads = (
        lax.all_to_all(query_rows, "sp", split_axis=2, concat_axis=1, tiled=True),
        lax.all_to_all(key_rows, "sp", split_axis=2, concat_axis=1, tiled=True),
        lax.all_to_all(value_rows, "sp", split_axis=2, concat_axis=1, tiled=True),
    )

    def head_view(values):
        return values.reshape(slot_count, full_rows, local_heads, HD)

    query_heads = head_view(query_heads)
    key_heads = head_view(key_heads)
    value_heads = head_view(value_heads)
    mixed_heads, log_total = lax.map(attend_slot, (query_heads, key_heads, value_heads, lengths))
    mixed_rows = lax.all_to_all(
        mixed_heads.reshape(slot_count, full_rows, 1, local_heads * HD),
        "sp",
        split_axis=1,
        concat_axis=2,
        tiled=True,
    )
    mixed_rows = mixed_rows.reshape(slot_count, row_count, width)
    middle = inputs + jnp.einsum(
        "nsd,de->nse", mixed_rows, w_out, preferred_element_type=jnp.float32
    )
    if post_norm:
        state_rows = norm_rows(middle, gain_att)
        ffn_in = state_rows.astype(jnp.bfloat16)
    else:
        state_rows = middle
        ffn_in = norm_rows(middle, gain_ffn).astype(jnp.bfloat16)
    gate_act = jnp.einsum("nsd,df->nsf", ffn_in, w_gate, preferred_element_type=jnp.float32)
    up_act = jnp.einsum("nsd,df->nsf", ffn_in, w_up, preferred_element_type=jnp.float32)
    hidden = gated(gate_act, up_act).astype(jnp.bfloat16)
    result = state_rows + jnp.einsum(
        "nsf,fd->nsd", hidden, w_down, preferred_element_type=jnp.float32
    )
    saved = (
        inputs,
        entry_rows,
        query_heads,
        key_heads,
        value_heads,
        log_total,
        mixed_rows,
        middle,
        ffn_in,
        gate_act,
        up_act,
        hidden,
        result,
    )
    if post_norm:
        return (norm_rows(result, gain_ffn), saved)
    return (result, saved)


def layer_backward(grad_output, saved, weights, lengths, post_norm, cosine, sine_table):
    w_query, w_key, w_value, w_out, w_gate, w_up, w_down, gain_att, gain_ffn = weights
    (
        inputs,
        entry_rows,
        query_heads,
        key_heads,
        value_heads,
        log_total,
        mixed_rows,
        middle,
        ffn_in,
        gate_act,
        up_act,
        hidden,
        result,
    ) = saved
    group = lax.axis_size("sp")
    slot_count, row_count, width = inputs.shape
    local_heads = HEADS // group
    full_rows = row_count * group
    if post_norm:
        discard, pull_result = jax.vjp(norm_rows, result, gain_ffn)
        grad_result, grad_gain_ffn = pull_result(grad_output)
    else:
        grad_result = grad_output
    grad_down_in = grad_result.astype(jnp.bfloat16)
    grad_w_down = jnp.einsum(
        "nsf,nsd->fd", hidden, grad_down_in, preferred_element_type=jnp.float32
    )
    grad_hidden = jnp.einsum(
        "nsd,fd->nsf", grad_down_in, w_down, preferred_element_type=jnp.float32
    )
    discard, pull_glu = jax.vjp(gated, gate_act, up_act)
    grad_gate, grad_up = pull_glu(grad_hidden)
    grad_gate = grad_gate.astype(jnp.bfloat16)
    grad_up = grad_up.astype(jnp.bfloat16)
    grad_w_gate = jnp.einsum("nsd,nsf->df", ffn_in, grad_gate, preferred_element_type=jnp.float32)
    grad_w_up = jnp.einsum("nsd,nsf->df", ffn_in, grad_up, preferred_element_type=jnp.float32)
    grad_ffn_in = jnp.einsum("nsf,df->nsd", grad_gate, w_gate, preferred_element_type=jnp.float32)
    grad_ffn_in = grad_ffn_in + jnp.einsum(
        "nsf,df->nsd", grad_up, w_up, preferred_element_type=jnp.float32
    )
    if post_norm:
        discard, pull_middle = jax.vjp(norm_rows, middle, gain_att)
        grad_middle, grad_gain_att = pull_middle(grad_result + grad_ffn_in)
    else:
        discard, pull_middle = jax.vjp(norm_rows, middle, gain_ffn)
        grad_normed, grad_gain_ffn = pull_middle(grad_ffn_in)
        grad_middle = grad_result + grad_normed
    grad_attn = grad_middle.astype(jnp.bfloat16)
    grad_w_out = jnp.einsum(
        "nsd,nse->de", mixed_rows, grad_attn, preferred_element_type=jnp.float32
    )
    grad_mixed = jnp.einsum(
        "nse,de->nsd", grad_attn, w_out, preferred_element_type=jnp.float32
    ).astype(jnp.bfloat16)
    grad_mixed = lax.all_to_all(
        grad_mixed.reshape(slot_count, row_count, group, local_heads * HD),
        "sp",
        split_axis=2,
        concat_axis=1,
        tiled=True,
    )
    grad_mixed = grad_mixed.reshape(slot_count, full_rows, local_heads, HD)
    grad_queries, grad_keys, grad_values = lax.map(
        attend_back, (query_heads, key_heads, value_heads, log_total, grad_mixed, lengths)
    )

    def head_pack(values):
        return values.reshape(slot_count, full_rows, 1, local_heads * HD)

    grad_query_rows, grad_key_rows, grad_value_rows = (
        lax.all_to_all(head_pack(grad_queries), "sp", split_axis=1, concat_axis=2, tiled=True),
        lax.all_to_all(head_pack(grad_keys), "sp", split_axis=1, concat_axis=2, tiled=True),
        lax.all_to_all(head_pack(grad_values), "sp", split_axis=1, concat_axis=2, tiled=True),
    )

    def unrotate(values):
        grads = values.astype(jnp.float32).reshape(slot_count, row_count, HEADS, HD)
        return (
            rotate_back(grads, cosine, sine_table)
            .astype(jnp.bfloat16)
            .reshape(slot_count, row_count, width)
        )

    grad_query_pre = unrotate(grad_query_rows)
    grad_key_pre = unrotate(grad_key_rows)
    grad_value_pre = grad_value_rows.reshape(slot_count, row_count, width)
    grad_w_query = jnp.einsum(
        "nsd,nse->de", entry_rows, grad_query_pre, preferred_element_type=jnp.float32
    )
    grad_w_key = jnp.einsum(
        "nsd,nse->de", entry_rows, grad_key_pre, preferred_element_type=jnp.float32
    )
    grad_w_value = jnp.einsum(
        "nsd,nse->de", entry_rows, grad_value_pre, preferred_element_type=jnp.float32
    )
    grad_entry = jnp.einsum(
        "nse,de->nsd", grad_query_pre, w_query, preferred_element_type=jnp.float32
    )
    grad_entry = grad_entry + jnp.einsum(
        "nse,de->nsd", grad_key_pre, w_key, preferred_element_type=jnp.float32
    )
    grad_entry = grad_entry + jnp.einsum(
        "nse,de->nsd", grad_value_pre, w_value, preferred_element_type=jnp.float32
    )
    if post_norm:
        grad_inputs = grad_middle + grad_entry
    else:
        discard, pull_inputs = jax.vjp(norm_rows, inputs, gain_att)
        grad_normed_in, grad_gain_att = pull_inputs(grad_entry)
        grad_inputs = grad_middle + grad_normed_in
    return (
        grad_inputs,
        (
            grad_w_query,
            grad_w_key,
            grad_w_value,
            grad_w_out,
            grad_w_gate,
            grad_w_up,
            grad_w_down,
            grad_gain_att,
            grad_gain_ffn,
        ),
    )


def body(
    tokens,
    lengths,
    post_query,
    post_key,
    post_value,
    post_out,
    post_gate,
    post_up,
    post_down,
    post_attn_gain,
    post_ffn_gain,
    pre_query,
    pre_key,
    pre_value,
    pre_out,
    pre_gate,
    pre_up,
    pre_down,
    pre_attn_gain,
    pre_ffn_gain,
    out_grad,
):
    slot_count, row_count, width = tokens.shape
    start = lax.axis_index("sp") * row_count
    cosine, sine_table = rotary_tables(start, row_count)
    layer_one = (
        post_query,
        post_key,
        post_value,
        post_out,
        post_gate,
        post_up,
        post_down,
        post_attn_gain,
        post_ffn_gain,
    )
    layer_two = (
        pre_query,
        pre_key,
        pre_value,
        pre_out,
        pre_gate,
        pre_up,
        pre_down,
        pre_attn_gain,
        pre_ffn_gain,
    )
    inputs_one = tokens.astype(jnp.float32)
    middle_state, saved_one = layer_forward(
        inputs_one, layer_one, lengths, True, cosine, sine_table
    )
    final_state, saved_two = layer_forward(
        middle_state, layer_two, lengths, False, cosine, sine_table
    )
    output = final_state.astype(jnp.bfloat16)
    positions = start + jnp.arange(row_count, dtype=jnp.int32)
    valid_rows = (positions[None, :] < lengths[:, None]).astype(jnp.float32)
    grad_final = out_grad.astype(jnp.float32) * valid_rows[:, :, None]
    grad_middle_state, grads_two = layer_backward(
        grad_final, saved_two, layer_two, lengths, False, cosine, sine_table
    )
    first_again, saved_one = layer_forward(inputs_one, layer_one, lengths, True, cosine, sine_table)
    grad_tokens, grads_one = layer_backward(
        grad_middle_state, saved_one, layer_one, lengths, True, cosine, sine_table
    )
    summed = lax.psum(
        (
            grads_one[0],
            grads_one[1],
            grads_one[2],
            grads_one[3],
            grads_one[4],
            grads_one[5],
            grads_one[6],
            grads_one[7],
            grads_one[8],
            grads_two[0],
            grads_two[1],
            grads_two[2],
            grads_two[3],
            grads_two[4],
            grads_two[5],
            grads_two[6],
            grads_two[7],
            grads_two[8],
        ),
        ("dp", "sp"),
    )
    grads_one = summed[:9]
    grads_two = summed[9:]
    tokens_grad = grad_tokens.astype(jnp.bfloat16)
    return (
        output,
        tokens_grad,
        grads_one[0],
        grads_one[1],
        grads_one[2],
        grads_one[3],
        grads_one[4],
        grads_one[5],
        grads_one[6],
        grads_one[7],
        grads_one[8],
        grads_two[0],
        grads_two[1],
        grads_two[2],
        grads_two[3],
        grads_two[4],
        grads_two[5],
        grads_two[6],
        grads_two[7],
        grads_two[8],
    )


def solution(mesh):
    in_specs = (
        P("dp", "sp", None),
        P("dp"),
        P(),
        P(),
        P(),
        P(),
        P(),
        P(),
        P(),
        P(),
        P(),
        P(),
        P(),
        P(),
        P(),
        P(),
        P(),
        P(),
        P(),
        P(),
        P("dp", "sp", None),
    )
    out_specs = (
        P("dp", "sp", None),
        P("dp", "sp", None),
        P(),
        P(),
        P(),
        P(),
        P(),
        P(),
        P(),
        P(),
        P(),
        P(),
        P(),
        P(),
        P(),
        P(),
        P(),
        P(),
        P(),
        P(),
    )
    return jax.shard_map(body, mesh=mesh, in_specs=in_specs, out_specs=out_specs, check_vma=False)
```

profile of v0, /device:TPU:0, one launch (start us, length us, event | category | flops | bytes accessed | tf_op | source)
XLA Modules:
  0.0 1286.7 jit_solution(16333060521162305157)
XLA Ops:
  9.9 4.2 all-to-all-start
  19.0 4.6 all-to-all-done
  28.9 6.9 all-to-all-done.1
  53.9 17.7 %while.62 = (s32[]{:T(128)}, bf16[2,1024,2,64]{1,3,2,0:T(8,128)(2,1)}, bf16[2,1024,2,64]{1,3,2,0:T(8,128)(2,1)}, s32[2]{0:T(128)S(1)}, bf16[2,1024,2,64]{1,3,2,0...) while((s32[]{:T(128)}, bf16[2,1024,2,64]{1,3,2,0:T(8,128)(2,1)}, ...), condition=%wide.region_3.4_spmd, body=%wide.region_0.3_spmd.sunk | while | flops 562166784 | bytes 36761784 | solution.py:129
  73.6 4.3 all-to-all-start.3
  78.8 17.7 %while.65 = (s32[]{:T(128)}, bf16[2,1024,2,64]{1,3,2,0:T(8,128)(2,1)}, f32[2,2,1024,1]{2,1,3,0:T(2,128)S(1)}, bf16[2,1024,2,64]{1,3,2,0:T(8,128)(2,1)}, s32[2]{0...) while((s32[]{:T(128)}, ...), condition=%wide.region_20.21_spmd, body=%wide.region_17.20_spmd.sunk | while | flops 562166784 | bytes 36769988 | solution.py:129
  98.8 4.1 all-to-all-start.12
  112.7 5.5 multiply_reduce_fusion.14
  125.0 4.4 all-to-all-start.4
  138.3 4.1 all-to-all-start.5
  145.0 6.4 all-to-all-done.5
  151.4 4.1 all-to-all-start.6
  169.8 17.7 %while.63 = (s32[]{:T(128)}, bf16[2,1024,2,64]{1,3,2,0:T(8,128)(2,1)}, f32[2,2,1024,1]{2,1,3,0:T(2,128)S(1)}, bf16[2,1024,2,64]{1,3,2,0:T(8,128)(2,1)}, s32[2]{0...) while((s32[]{:T(128)}, ...), condition=%wide.region_10.11_spmd, body=%wide.region_7.10_spmd.sunk | while | flops 562166784 | bytes 36769988 | solution.py:129
  189.5 4.5 all-to-all-start.7
  194.1 5.3 multiply_convert_fusion.3
  219.8 4.3 all-to-all-start.8
  228.0 5.0 all-to-all-done.8
  239.8 28.9 %while.64 = (s32[]{:T(128)}, bf16[2,1024,2,64]{1,3,2,0:T(8,128)(2,1)}, bf16[2,1024,2,64]{1,3,2,0:T(8,128)(2,1)}, bf16[2,1024,2,64]{1,3,2,0:T(8,128)(2,1)}, bf16[...) while((s32[]{:T(128)}, ...), condition=%wide.region_15.16_spmd, body=%wide.region_13.15_spmd.sunk | while | flops 1376386048 | bytes 86572392 | solution.py:238
  283.2 4.1 all-to-all-start.9
  332.9 4.5 all-to-all-start.13
  353.3 28.9 %while.66 = (s32[]{:T(128)}, bf16[2,1024,2,64]{1,3,2,0:T(8,128)(2,1)}, bf16[2,1024,2,64]{1,3,2,0:T(8,128)(2,1)}, bf16[2,1024,2,64]{1,3,2,0:T(8,128)(2,1)}, bf16[...) while((s32[]{:T(128)}, ...), condition=%wide.region_27.28_spmd, body=%wide.region_25.27_spmd.sunk | while | flops 1376386048 | bytes 86572392 | solution.py:238
  390.3 4.2 convolution_bitcast_fusion.5
  436.4 43.2 %all-reduce = (f32[512]{0:T(512)}, f32[512]{0:T(512)}, f32[512]{0:T(512)}, f32[512]{0:T(512)}) all-reduce(f32[512]{0:T(512)S(1)} %get-tuple-element.373, f32[512]{0:T(512)S(1)} %get-tuple-element.371, f32[512]{0:T(512)S(1)} %get-tuple-element.367, f32[512]{0:T(512)S(1)} %copy-done.112), channel_id=1, replica_groups=mesh['dp'=8,'sp'=4] {'dp','sp'}, use_global_device_ids=true, to_apply=%region_36.37 | all-reduce | flops 2048 | bytes 16384 | tf_op jit(solution)/shard_map/psum | solution.py:368
  485.2 765.8 %all-reduce.4.cloned.1.call-done = (f32[512,512]{0,1:T(8,128)}, f32[512,512]{0,1:T(8,128)}, f32[512,512]{0,1:T(8,128)}, f32[512,512]{1,0:T(8,128)}, f32[512,1376...) async-done(((f32[512,512]{0,1:T(8,128)}, ...) | async-done | bytes 25296912 | tf_op jit(solution)/shard_map/psum | solution.py:368
  (568 shorter events, 380.4 us)
Async XLA Ops:
  7.2 203.1 %copy-start = (bf16[512,1376]{0,1:T(8,128)(2,1)S(1)}, bf16[512,1376]{0,1:T(8,128)(2,1)}, u32[]{:S(2)}) copy-start(bf16[512,1376]{0,1:T(8,128)(2,1)} %param.46) | copy-start | bytes 4227076
  9.9 13.7 %all-to-all-start = ((bf16[2,256,4,128]{3,1,0,2:T(8,128)(2,1)}), bf16[2,256,4,128]{3,1,0,2:T(8,128)(2,1)}, u32[]{:S(2)}, u32[]{:S(2)}) async-start(bf16[2,256,4,128]{3,1,0,2:T(8,128)(2,1)} %bitcast.523), calls=%async_computation | async-start | bytes 1048576 | tf_op jit(solution)/shard_map/all_to_all | solution.py:120
  16.9 114.0 %copy-start.12 = (f32[256,8,64]{0,2,1:T(8,128)}, f32[256,8,64]{0,2,1:T(8,128)S(1)}, u32[]{:S(2)}) copy-start(f32[256,8,64]{0,2,1:T(8,128)S(1)} %mul.533) | copy-start | bytes 1572868
  18.1 21.2 %copy-start.113 = (s32[2]{0:T(128)S(1)}, s32[2]{0:T(128)}, u32[]{:S(2)}) copy-start(s32[2]{0:T(128)} %param.32) | copy-start | bytes 28
  23.6 12.3 all-to-all-start.1
  35.9 14.6 %all-to-all-start.2 = ((bf16[2,256,4,128]{1,3,0,2:T(8,128)(2,1)}), bf16[2,256,4,128]{1,3,0,2:T(8,128)(2,1)S(1)}, u32[]{:S(2)}, u32[]{:S(2)}) async-start(bf16[2,256,4,128]{1,3,0,2:T(8,128)(2,1)} %copy.334), calls=%async_computation.2 | async-start | bytes 1048576 | tf_op jit(solution)/shard_map/all_to_all | solution.py:119
  73.6 25.2 %all-to-all-start.3 = ((bf16[2,1024,1,128]{3,0,2,1:T(2,128)(2,1)}), bf16[2,1024,1,128]{3,0,2,1:T(2,128)(2,1)}, u32[]{:S(2)}, u32[]{:S(2)}) async-start(bf16[2,1024,1,128]{3,0,2,1:T(2,128)(2,1)} %copy.336), calls=%async_computation.3 | async-start | bytes 1048576 | tf_op jit(solution)/shard_map/all_to_all | solution.py:130
  98.8 26.3 %all-to-all-start.12 = ((bf16[2,1024,1,128]{3,0,2,1:T(2,128)(2,1)}), bf16[2,1024,1,128]{3,0,2,1:T(2,128)(2,1)}, u32[]{:S(2)}, u32[]{:S(2)}) async-start(bf16[2,1024,1,128]{3,0,2,1:T(2,128)(2,1)} %copy.367), calls=%async_computation.12 | async-start | bytes 1048576 | tf_op jit(solution)/shard_map/all_to_all | solution.py:130
  125.0 13.3 %all-to-all-start.4 = ((bf16[2,256,4,128]{3,1,0,2:T(8,128)(2,1)}), bf16[2,256,4,128]{3,1,0,2:T(8,128)(2,1)}, u32[]{:S(2)}, u32[]{:S(2)}) async-start(bf16[2,256,4,128]{3,1,0,2:T(8,128)(2,1)} %bitcast.646), calls=%async_computation.4 | async-start | bytes 1048576 | tf_op jit(solution)/shard_map/all_to_all | solution.py:120
  138.3 18.6 %copy-start.36 = (bf16[2,256,512]{2,1,0:T(8,128)(2,1)}, bf16[2,256,512]{2,1,0:T(8,128)(2,1)S(1)}, u32[]{:S(2)}) copy-start(bf16[2,256,512]{2,1,0:T(8,128)(2,1)S(1)} %reshape.627) | copy-start | bytes 1572868
  138.3 13.1 %all-to-all-start.5 = ((bf16[2,256,4,128]{1,3,0,2:T(8,128)(2,1)}), bf16[2,256,4,128]{1,3,0,2:T(8,128)(2,1)}, u32[]{:S(2)}, u32[]{:S(2)}) async-start(bf16[2,256,4,128]{1,3,0,2:T(8,128)(2,1)} %copy.343), calls=%async_computation.5 | async-start | bytes 1048576 | tf_op jit(solution)/shard_map/all_to_all | solution.py:118
  144.9 16.0 %copy-start.109 = (f32[2,256]{1,0:T(2,128)}, f32[2,256]{1,0:T(2,128)S(1)}, u32[]{:S(2)}) copy-start(f32[2,256]{1,0:T(2,128)S(1)} %get-tuple-element.529) | copy-start | bytes 6148
  151.4 13.9 %all-to-all-start.6 = ((bf16[2,256,4,128]{1,3,0,2:T(8,128)(2,1)}), bf16[2,256,4,128]{1,3,0,2:T(8,128)(2,1)}, u32[]{:S(2)}, u32[]{:S(2)}) async-start(bf16[2,256,4,128]{1,3,0,2:T(8,128)(2,1)} %copy.347), calls=%async_computation.6 | async-start | bytes 1048576 | tf_op jit(solution)/shard_map/all_to_all | solution.py:119
  189.5 13.4 %all-to-all-start.7 = ((bf16[2,1024,1,128]{3,0,2,1:T(2,128)(2,1)}), bf16[2,1024,1,128]{3,0,2,1:T(2,128)(2,1)}, u32[]{:S(2)}, u32[]{:S(2)}) async-start(bf16[2,1024,1,128]{3,0,2,1:T(2,128)(2,1)} %copy.349), calls=%async_computation.7 | async-start | bytes 1048576 | tf_op jit(solution)/shard_map/all_to_all | solution.py:130
  219.8 13.2 %all-to-all-start.8 = ((bf16[2,256,4,128]{3,1,0,2:T(8,128)(2,1)}), bf16[2,256,4,128]{3,1,0,2:T(8,128)(2,1)}, u32[]{:S(2)}, u32[]{:S(2)}) async-start(bf16[2,256,4,128]{3,1,0,2:T(8,128)(2,1)} %bitcast.657), calls=%async_computation.8 | async-start | bytes 1048576 | tf_op jit(solution)/shard_map/all_to_all | solution.py:230
  270.7 12.5 all-to-all-start.10
  283.2 13.1 %all-to-all-start.9 = ((bf16[2,1024,1,128]{3,0,2,1:T(2,128)(2,1)}), bf16[2,1024,1,128]{3,0,2,1:T(2,128)(2,1)}, u32[]{:S(2)}, u32[]{:S(2)}) async-start(bf16[2,1024,1,128]{3,0,2,1:T(2,128)(2,1)} %copy.354), calls=%async_computation.9 | async-start | bytes 1048576 | tf_op jit(solution)/shard_map/all_to_all | solution.py:246
  296.3 15.1 %all-to-all-start.11 = ((bf16[2,1024,1,128]{3,0,2,1:T(2,128)(2,1)}), bf16[2,1024,1,128]{3,0,2,1:T(2,128)(2,1)S(1)}, u32[]{:S(2)}, u32[]{:S(2)}) async-start(bf16[2,1024,1,128]{3,0,2,1:T(2,128)(2,1)} %copy.364), calls=%async_computation.11 | async-start | bytes 1048576 | tf_op jit(solution)/shard_map/all_to_all | solution.py:248
  332.9 13.5 %all-to-all-start.13 = ((bf16[2,256,4,128]{3,1,0,2:T(8,128)(2,1)}), bf16[2,256,4,128]{3,1,0,2:T(8,128)(2,1)}, u32[]{:S(2)}, u32[]{:S(2)}) async-start(bf16[2,256,4,128]{3,1,0,2:T(8,128)(2,1)} %bitcast.649), calls=%async_computation.13 | async-start | bytes 1048576 | tf_op jit(solution)/shard_map/all_to_all | solution.py:230
  384.2 12.4 all-to-all-start.15
  397.4 12.3 all-to-all-start.14
  410.5 12.3 all-to-all-start.16
  414.0 837.0 %all-reduce.4.cloned.1.call-start = ((), (), s32[]{:S(2)}) async-start(), calls=%async_computation.17 | async-start | bytes 50593792 | tf_op jit(solution)/shard_map/psum | solution.py:368
  432.8 48.5 %copy-start.43 = (bf16[2,256,512]{1,2,0:T(8,128)(2,1)S(1)}, bf16[2,256,512]{1,2,0:T(8,128)(2,1)}, u32[]{:S(2)}) copy-start(bf16[2,256,512]{1,2,0:T(8,128)(2,1)} %copy-done.42) | copy-start | bytes 1572868
  (139 other events, 463.9 us)
Sparse Core Ops, SparseCore 0:
  431.7 819.2 all-reduce.3
where the time goes:
time: 1300 us; the launch traced here: 1290 us
  waiting for transfers between devices  797 us (61%)
  matrix products  157 us (12%)
  local copies, waits for them, and re-layouts  147 us (11%)
  starting transfers between devices  67.6 us (5%)
  other arithmetic  57.9 us (4%)
  blocking collectives  43.2 us (3%)
  between operations  15.6 us (1%)
    psum x1, waiting for transfers between devices, body(): lax.psum((grads_one[0], grads_one[1], grads_one[2], grads_one[3], grads_o...  766 us
    unnamed x204, local copies, waits for them, and re-layouts  44.3 us
    psum x1, blocking collectives, body(): lax.psum((grads_one[0], grads_one[1], grads_one[2], grads_one[3], grads_o...  43.2 us
  transfers between devices with their start and end apart: 18, of which 12 were waited for; matrix products, arithmetic and copies ran while one was open for 12% of the time, Pallas kernels for 0%

commit v1 on v0

--- a/solution.py
+++ b/solution.py
@@ -366,27 +366,30 @@
         grad_middle_state, saved_one, layer_one, lengths, True, cosine, sine_table
     )
     summed = lax.psum(
-        (
-            grads_one[0],
-            grads_one[1],
-            grads_one[2],
-            grads_one[3],
-            grads_one[4],
-            grads_one[5],
-            grads_one[6],
-            grads_one[7],
-            grads_one[8],
-            grads_two[0],
-            grads_two[1],
-            grads_two[2],
-            grads_two[3],
-            grads_two[4],
-            grads_two[5],
-            grads_two[6],
-            grads_two[7],
-            grads_two[8],
+        lax.psum(
+            (
+                grads_one[0],
+                grads_one[1],
+                grads_one[2],
+                grads_one[3],
+                grads_one[4],
+                grads_one[5],
+                grads_one[6],
+                grads_one[7],
+                grads_one[8],
+                grads_two[0],
+                grads_two[1],
+                grads_two[2],
+                grads_two[3],
+                grads_two[4],
+                grads_two[5],
+                grads_two[6],
+                grads_two[7],
+                grads_two[8],
+            ),
+            "sp",
         ),
-        ("dp", "sp"),
+        "dp",
     )
     grads_one = summed[:9]
     grads_two = summed[9:]

time: 1300 us -> 1690 us (1.30)
  waiting for transfers between devices: 797 us -> 1210 us
    psum x0 -> x1, waiting for transfers between devices: none -> 740 us  [body(): lax.psum(lax.psum((grads_one[0], grads_one[1], grads_one[2], grads_one[3]...]
    psum x1, waiting for transfers between devices: 766 us -> 436 us  [body(): lax.psum((grads_one[0], grads_one[1], grads_one[2], grads_one[3], grads_o...]
    psum x1, blocking collectives: 43.2 us -> 6.11 us  [body(): lax.psum((grads_one[0], grads_one[1], grads_one[2], grads_one[3], grads_o...]
    psum x0 -> x1, blocking collectives: none -> 23.4 us  [body(): lax.psum(lax.psum((grads_one[0], grads_one[1], grads_one[2], grads_one[3]...]
    unnamed x204 -> x212, local copies, waits for them, and re-layouts: 44.3 us -> 40.6 us
  transfers between devices with their start and end apart: 18 -> 19, of which waited for: 12 -> 13; matrix products, arithmetic and copies ran while one was open for 12% -> 9% of each run, Pallas kernels for 0% -> 0%
where the time goes in v1:
time: 1690 us; the launch traced here: 1680 us
  waiting for transfers between devices  1210 us (72%)
  matrix products  157 us (9%)
  local copies, waits for them, and re-layouts  145 us (9%)
  starting transfers between devices  68.3 us (4%)
  other arithmetic  58 us (3%)
  blocking collectives  29.5 us (2%)
    psum x1, waiting for transfers between devices, body(): lax.psum(lax.psum((grads_one[0], grads_one[1], grads_one[2], grads_one[3]...  740 us
    psum x1, waiting for transfers between devices, body(): lax.psum((grads_one[0], grads_one[1], grads_one[2], grads_one[3], grads_o...  436 us
    unnamed x212, local copies, waits for them, and re-layouts  40.6 us
  transfers between devices with their start and end apart: 19, of which 13 were waited for; matrix products, arithmetic and copies ran while one was open for 9% of the time, Pallas kernels for 0%

profile of v1, /device:TPU:0, one launch (start us, length us, event | category | flops | bytes accessed | tf_op | source)
XLA Modules:
  0.0 1682.9 jit_solution(10783165043552597633)
XLA Ops:
  9.9 4.2 all-to-all-start
  19.0 4.6 all-to-all-done
  28.9 6.9 all-to-all-done.1
  53.9 17.7 %while.62 = (s32[]{:T(128)}, bf16[2,1024,2,64]{1,3,2,0:T(8,128)(2,1)}, bf16[2,1024,2,64]{1,3,2,0:T(8,128)(2,1)}, s32[2]{0:T(128)S(1)}, bf16[2,1024,2,64]{1,3,2,0...) while((s32[]{:T(128)}, bf16[2,1024,2,64]{1,3,2,0:T(8,128)(2,1)}, ...), condition=%wide.region_3.4_spmd, body=%wide.region_0.3_spmd.sunk | while | flops 562166784 | bytes 36761784 | solution.py:129
  73.6 4.3 all-to-all-start.3
  78.7 17.7 %while.65 = (s32[]{:T(128)}, bf16[2,1024,2,64]{1,3,2,0:T(8,128)(2,1)}, f32[2,2,1024,1]{2,1,3,0:T(2,128)S(1)}, bf16[2,1024,2,64]{1,3,2,0:T(8,128)(2,1)}, s32[2]{0...) while((s32[]{:T(128)}, ...), condition=%wide.region_20.21_spmd, body=%wide.region_17.20_spmd.sunk | while | flops 562166784 | bytes 36769988 | solution.py:129
  112.7 5.4 multiply_reduce_fusion.14
  125.0 4.4 all-to-all-start.4
  138.3 4.2 all-to-all-start.5
  144.9 6.4 all-to-all-done.5
  169.8 17.7 %while.63 = (s32[]{:T(128)}, bf16[2,1024,2,64]{1,3,2,0:T(8,128)(2,1)}, f32[2,2,1024,1]{2,1,3,0:T(2,128)S(1)}, bf16[2,1024,2,64]{1,3,2,0:T(8,128)(2,1)}, s32[2]{0...) while((s32[]{:T(128)}, ...), condition=%wide.region_10.11_spmd, body=%wide.region_7.10_spmd.sunk | while | flops 562166784 | bytes 36769988 | solution.py:129
  189.5 4.5 all-to-all-start.7
  194.1 5.3 multiply_convert_fusion.3
  219.7 4.3 all-to-all-start.8
  228.0 5.0 all-to-all-done.8
  239.8 28.9 %while.64 = (s32[]{:T(128)}, bf16[2,1024,2,64]{1,3,2,0:T(8,128)(2,1)}, bf16[2,1024,2,64]{1,3,2,0:T(8,128)(2,1)}, bf16[2,1024,2,64]{1,3,2,0:T(8,128)(2,1)}, bf16[...) while((s32[]{:T(128)}, ...), condition=%wide.region_15.16_spmd, body=%wide.region_13.15_spmd.sunk | while | flops 1376386048 | bytes 86572392 | solution.py:238
  283.2 4.1 all-to-all-start.9
  334.5 4.5 all-to-all-start.13
  354.8 28.9 %while.66 = (s32[]{:T(128)}, bf16[2,1024,2,64]{1,3,2,0:T(8,128)(2,1)}, bf16[2,1024,2,64]{1,3,2,0:T(8,128)(2,1)}, bf16[2,1024,2,64]{1,3,2,0:T(8,128)(2,1)}, bf16[...) while((s32[]{:T(128)}, ...), condition=%wide.region_27.28_spmd, body=%wide.region_25.27_spmd.sunk | while | flops 1376386048 | bytes 86572392 | solution.py:238
  391.9 4.2 convolution_bitcast_fusion.5
  434.9 436.3 %all-reduce.9.cloned.1.call-done = (f32[512,512]{0,1:T(8,128)}, f32[512,512]{0,1:T(8,128)}, f32[512,512]{0,1:T(8,128)}, f32[512,512]{1,0:T(8,128)}, f32[512,1376...) async-done(((f32[512,512]{0,1:T(8,128)}, ...) | async-done | bytes 25296912 | tf_op jit(solution)/shard_map/psum | solution.py:369
  876.1 6.1 all-reduce.2
  882.2 23.4 %all-reduce = (f32[512]{0:T(512)}, f32[512]{0:T(512)}, f32[512]{0:T(512)}, f32[512]{0:T(512)}) all-reduce(f32[512]{0:T(512)S(1)} %get-tuple-element.473, f32[512]{0:T(512)S(1)} %get-tuple-element.474, f32[512]{0:T(512)S(1)} %get-tuple-element.475, f32[512]{0:T(512)S(1)} %get-tuple-element.476), channel_id=1, replica_groups=mesh['dp'=8,'sp'=4] {'dp'}, use_global_device_ids=true, to_apply=%region_44.45 | all-reduce | flops 2048 | bytes 16384 | tf_op jit(solution)/shard_map/psum | solution.py:368
  910.1 739.8 %all-reduce.7.cloned.1.call-done = (f32[512,512]{0,1:T(8,128)}, f32[512,512]{0,1:T(8,128)}, f32[512,512]{0,1:T(8,128)}, f32[512,512]{1,0:T(8,128)}, f32[512,1376...) async-done(((f32[512,512]{0,1:T(8,128)}, ...) | async-done | bytes 25296912 | tf_op jit(solution)/shard_map/psum | solution.py:368
  (580 shorter events, 388.3 us)
Async XLA Ops:
  7.2 203.1 %copy-start = (bf16[512,1376]{0,1:T(8,128)(2,1)S(1)}, bf16[512,1376]{0,1:T(8,128)(2,1)}, u32[]{:S(2)}) copy-start(bf16[512,1376]{0,1:T(8,128)(2,1)} %param.46) | copy-start | bytes 4227076
  9.9 13.7 all-to-all-start
  16.9 113.9 %copy-start.12 = (f32[256,8,64]{0,2,1:T(8,128)}, f32[256,8,64]{0,2,1:T(8,128)S(1)}, u32[]{:S(2)}) copy-start(f32[256,8,64]{0,2,1:T(8,128)S(1)} %mul.533) | copy-start | bytes 1572868
  18.1 21.2 %copy-start.117 = (s32[2]{0:T(128)S(1)}, s32[2]{0:T(128)}, u32[]{:S(2)}) copy-start(s32[2]{0:T(128)} %param.32) | copy-start | bytes 28
  23.6 12.3 all-to-all-start.1
  35.9 14.6 all-to-all-start.2
  73.6 25.2 %all-to-all-start.3 = ((bf16[2,1024,1,128]{3,0,2,1:T(2,128)(2,1)}), bf16[2,1024,1,128]{3,0,2,1:T(2,128)(2,1)}, u32[]{:S(2)}, u32[]{:S(2)}) async-start(bf16[2,1024,1,128]{3,0,2,1:T(2,128)(2,1)} %copy.336), calls=%async_computation.3 | async-start | bytes 1048576 | tf_op jit(solution)/shard_map/all_to_all | solution.py:130
  98.7 26.3 %all-to-all-start.12 = ((bf16[2,1024,1,128]{3,0,2,1:T(2,128)(2,1)}), bf16[2,1024,1,128]{3,0,2,1:T(2,128)(2,1)}, u32[]{:S(2)}, u32[]{:S(2)}) async-start(bf16[2,1024,1,128]{3,0,2,1:T(2,128)(2,1)} %copy.367), calls=%async_computation.12 | async-start | bytes 1048576 | tf_op jit(solution)/shard_map/all_to_all | solution.py:130
  125.0 13.3 all-to-all-start.4
  138.3 13.1 all-to-all-start.5
  151.4 13.9 all-to-all-start.6
  189.5 13.4 all-to-all-start.7
  219.7 13.2 all-to-all-start.8
  270.7 12.5 all-to-all-start.10
  283.2 13.1 all-to-all-start.9
  296.3 15.5 all-to-all-start.11
  334.5 13.5 all-to-all-start.13
  385.7 12.4 all-to-all-start.15
  399.0 12.3 all-to-all-start.14
  412.1 12.3 all-to-all-start.16
  415.5 455.7 %all-reduce.9.cloned.1.call-start = ((), (), s32[]{:S(2)}) async-start(), calls=%async_computation.18 | async-start | bytes 50593792 | tf_op jit(solution)/shard_map/psum | solution.py:369
  434.9 1215.0 %all-reduce.7.cloned.1.call-start = ((), (), s32[]{:S(2)}) async-start(), calls=%async_computation.17 | async-start | bytes 50593792 | tf_op jit(solution)/shard_map/psum | solution.py:368
  872.5 34.8 %copy-start.42 = (bf16[2,256,512]{1,2,0:T(8,128)(2,1)S(1)}, bf16[2,256,512]{1,2,0:T(8,128)(2,1)}, u32[]{:S(2)}) copy-start(bf16[2,256,512]{1,2,0:T(8,128)(2,1)} %copy-done.41) | copy-start | bytes 1572868
  876.1 32.7 %copy-start.55 = (bf16[512,512]{1,0:T(8,128)(2,1)S(1)}, bf16[512,512]{1,0:T(8,128)(2,1)}, u32[]{:S(2)}) copy-start(bf16[512,512]{1,0:T(8,128)(2,1)} %param.35) | copy-start | bytes 1572868
  (144 other events, 510.9 us)
Sparse Core Ops, SparseCore 0:
  435.0 436.1 all-reduce.8
  877.7 772.2 all-reduce.6
